TPU v7x, 32 devices: a whole 2x2x4 slice. The times are simulated.
32 devices in a mesh: req: 8 (over z, x), head: 4 (over y, core).
Axes of the slice: x: 2, y: 2, z: 4, core: 2. Of those that a mesh axis runs over, the one named last changes fastest.
Arguments:
- resid: bfloat16 [32, 4, 2048], P('req'), may hold values from -6 to 6
- proj: bfloat16 [32, 4, 3, 2048], P('req', None, None, 'head'), may hold values from -6 to 6
- conv_cache: bfloat16 [32, 3, 3, 2048], P('req', None, None, 'head'), may hold values from -6 to 6
- conv_weight: bfloat16 [4, 3, 2048], P(None, None, 'head'), may hold values from -3 to 3
- forget_bias: float32 [2048], P('head'), may hold values from -2 to 6
- owner: int32 [32], replicated, may hold values from 0 to 31, each once
- lengths: int32 [32], replicated, may hold values from 0 to 4096, as said below
- old_state: bfloat16 [32, 16, 128, 128], P('req', 'head'), may hold values from -6 to 6
- norm_gain: float32 [2048], P('head'), may hold values from 0.5 to 1.5
- out_weight: bfloat16 [2048, 2048], P('head'), may hold values from -0.125 to 0.125
Outputs:
- mixed: bfloat16 [32, 4, 2048], P('req')
- new_state: bfloat16 [32, 16, 128, 128], P('req', 'head')
Inputs may be any that keep to these rules, and one draw needn't show every extreme that they name: `lengths`: short requests (below 3) and long ones are mixed; some request has length 0 and some 4096.
All inputs are finite; a program needn't handle non-finite values.
Results may differ from a plain program's by a relative error of at most 0.015.
Values may be sent and summed in bfloat16 or wider, within the bound.
No kernel may reach another device: no remote copies, remote signals or barrier semaphores. Data moves between devices by JAX's collectives and lax.ppermute only.
A program may use at most 64 MiB of HBM per device.

v0:
```python
import jax
import jax.numpy as jnp
from jax import lax
from jax.sharding import PartitionSpec as P


def convolve(proj, conv_cache, conv_weight, lens):
    taps = conv_weight.shape[0]
    new_tokens = proj.shape[1]
    joined = jnp.concatenate([conv_cache, proj], axis=1).astype(jnp.float32)
    places = lens[:, None] + jnp.arange(-(taps - 1), new_tokens, dtype=jnp.int32)[None, :]
    joined = jnp.where((places >= 0)[:, :, None, None], joined, jnp.float32(0.0))
    summed = jnp.zeros(proj.shape, jnp.float32)
    for offset in range(taps):
        begin_at = taps - 1 - offset
        summed = summed + joined[:, begin_at : begin_at + new_tokens] * conv_weight[offset].astype(
            jnp.float32
        )
    return jax.nn.silu(summed).astype(jnp.bfloat16)


def recurrence(convolved, relocated, lens, forget_bias, norm_gain, head_size):
    local_reqs, new_tokens, _, channels = convolved.shape
    head_count = channels // head_size
    values = convolved.astype(jnp.float32).reshape(local_reqs, new_tokens, 3, head_count, head_size)
    queries = values[:, :, 0]
    keep_rate = jax.nn.sigmoid(values[:, :, 1] + forget_bias.reshape(head_count, head_size))
    inputs = values[:, :, 2]
    current = relocated.astype(jnp.float32) * (lens > 0).astype(jnp.float32)[:, None, None, None]
    outputs = []
    for position in range(new_tokens):
        rate_now = keep_rate[:, position]
        current = (
            rate_now[..., None] * current
            + (1.0 - rate_now)[..., None] * inputs[:, position][:, :, None, :]
        )
        outputs.append(jnp.einsum("rhk,rhkv->rhv", queries[:, position], current))
    stacked = jnp.stack(outputs, axis=1)
    inverse_rms = lax.rsqrt(jnp.mean(stacked * stacked, axis=-1, keepdims=True) + 1e-06)
    normed = (stacked * inverse_rms).reshape(local_reqs, new_tokens, channels) * norm_gain
    return (normed.astype(jnp.bfloat16), current.astype(jnp.bfloat16))


def body(
    resid,
    proj,
    conv_cache,
    conv_weight,
    forget_bias,
    owner,
    lengths,
    old_state,
    norm_gain,
    out_weight,
):
    local_reqs = resid.shape[0]
    new_tokens = resid.shape[1]
    devices = lax.axis_size("req")
    own_index = lax.axis_index("req")
    total_reqs = owner.shape[0]
    head_size = old_state.shape[-1]
    inverse = (
        jnp.zeros((total_reqs,), jnp.int32).at[owner].set(jnp.arange(total_reqs, dtype=jnp.int32))
    )
    local_lens = lax.dynamic_slice_in_dim(lengths, own_index * local_reqs, local_reqs)
    convolved = convolve(proj, conv_cache, conv_weight, local_lens)
    pieces = old_state.reshape(local_reqs, devices, -1)
    spread = lax.all_to_all(pieces, "req", split_axis=1, concat_axis=0, tiled=True).reshape(
        total_reqs, -1
    )
    picked = jnp.take(spread, inverse, axis=0).reshape(devices, local_reqs, 1, -1)
    routed = lax.all_to_all(picked, "req", split_axis=0, concat_axis=2, tiled=True)
    relocated = routed.reshape(old_state.shape)
    normed, new_state = recurrence(
        convolved, relocated, local_lens, forget_bias, norm_gain, head_size
    )
    flat_normed = normed.reshape(local_reqs * new_tokens, -1)
    flat_resid = resid.reshape(local_reqs * new_tokens, -1)
    partial_value = jnp.dot(flat_normed, out_weight, preferred_element_type=jnp.float32)
    summed = lax.psum(partial_value, "head")
    mixed = (flat_resid.astype(jnp.float32) + summed).astype(jnp.bfloat16).reshape(resid.shape)
    return (mixed, new_state)


def solution(mesh):
    in_specs = (
        P("req", None, None),
        P("req", None, None, "head"),
        P("req", None, None, "head"),
        P(None, None, "head"),
        P("head"),
        P(),
        P(),
        P("req", "head", None, None),
        P("head"),
        P("head", None),
    )
    out_specs = (P("req", None, None), P("req", "head", None, None))
    return jax.shard_map(body, mesh=mesh, in_specs=in_specs, out_specs=out_specs, check_vma=False)
```

profile of v0, /device:TPU:0, one launch (start us, length us, event | category | flops | bytes accessed | tf_op | source)
XLA Modules:
  0.0 103.1 jit_solution(8104832526261652992)
XLA Ops:
  7.2 0.0 copy-start
  7.2 0.0 copy-start.4
  7.2 0.0 copy-start.3
  7.2 0.0 copy-start.7
  7.2 0.0 copy-start.2
  7.2 0.0 copy-start.8
  7.2 0.0 copy-start.5
  7.2 1.4 %reshape.167 = bf16[4,8,8192]{2,1,0:T(8,128)(2,1)S(1)} reshape(bf16[4,4,128,128]{3,2,1,0:T(8,128)(2,1)} %param.17) | data formatting | bytes 1048576 | tf_op jit(solution)/shard_map/reshape | solution.py:67
  8.6 1.2 %copy.27 = bf16[4,8,8192]{2,0,1:T(4,128)(2,1)} copy(bf16[4,8,8192]{2,1,0:T(8,128)(2,1)S(1)} %reshape.167) | data formatting | bytes 1048576 | tf_op jit(solution)/shard_map/reshape | solution.py:67
  9.8 7.3 %all-to-all-start = ((bf16[4,8,8192]{2,0,1:T(4,128)(2,1)}), bf16[4,8,8192]{2,0,1:T(4,128)(2,1)S(1)}, u32[]{:S(2)}, u32[]{:S(2)}) async-start(bf16[4,8,8192]{2,0,1:T(4,128)(2,1)} %copy.27), calls=%async_computation | async-start | bytes 1048576 | tf_op jit(solution)/shard_map/all_to_all | solution.py:68
  17.1 0.0 copy-done.4
  17.1 0.0 copy-done.3
  17.2 0.0 copy-done.7
  17.2 0.1 compare_convert_fusion
  17.3 0.1 add_compare_fusion
  17.4 0.0 copy-done.2
  17.4 0.1 convert_select_fusion
  17.5 0.1 fusion.21
  17.6 0.0 copy-done.8
  17.7 0.7 scatter_custom_fusion
  18.4 0.1 broadcast_in_dim.46
  18.5 0.0 copy-done.5
  18.6 13.0 %all-to-all-done = bf16[4,8,8192]{2,0,1:T(4,128)(2,1)S(1)} async-done(((bf16[4,8,8192]{2,0,1:T(4,128)(2,1)}), bf16[4,8,8192]{2,0,1:T(4,128)(2,1)S(1)}, u32[]{:S(2)}, u32[]{:S(2)}) %all-to-all-start) | async-done | bytes 524320 | tf_op jit(solution)/shard_map/all_to_all | solution.py:68
  31.6 0.1 reshape.168
  31.7 0.9 gather_fusion
  32.6 0.0 copy-start.1
  32.6 0.2 gather.7
  32.8 1.1 %bitcast_select_fusion = bf16[8,4,1,8192]{3,1,2,0:T(4,128)(2,1)} fusion(bf16[8,4,1,8192]{3,1,0,2:T(4,128)(2,1)S(1)} %gather.7, pred[8,4]{1,0:T(8,128)(4,1)S(1)} %broadcast_in_dim.46), kind=kLoop, calls=%fused_computation.11 | loop fusion | flops 262144 | bytes 1048608 | tf_op jit(solution)/shard_map/jit(_take)/select_n | solution.py:71
  33.9 3.6 %all-to-all-start.1 = ((bf16[8,4,1,8192]{3,1,2,0:T(4,128)(2,1)}), bf16[8,4,1,8192]{3,1,2,0:T(4,128)(2,1)S(1)}, u32[]{:S(2)}, u32[]{:S(2)}) async-start(bf16[8,4,1,8192]{3,1,2,0:T(4,128)(2,1)} %bitcast_select_fusion), calls=%async_computation.1 | async-start | bytes 1048576 | tf_op jit(solution)/shard_map/all_to_all | solution.py:72
  37.5 0.0 all-reduce.2.cloned.1.call-start
  37.6 0.0 copy-done.1
  37.7 14.5 %all-to-all-done.1 = bf16[8,4,1,8192]{3,1,2,0:T(4,128)(2,1)S(1)} async-done(((bf16[8,4,1,8192]{3,1,2,0:T(4,128)(2,1)}), bf16[8,4,1,8192]{3,1,2,0:T(4,128)(2,1)S(1)}, u32[]{:S(2)}, u32[]{:S(2)}) %all-to-all-start.1) | async-done | bytes 524320 | tf_op jit(solution)/shard_map/all_to_all | solution.py:72
  52.2 0.1 convert_bitcast_fusion
  52.3 1.6 %copy.29 = f32[1,4,8,1,8192]{4,2,1,3,0:T(8,128)} copy(f32[1,4,8,1,8192]{4,1,2,3,0:T(4,128)S(1)} %convert_bitcast_fusion) | data formatting | bytes 2097152 | tf_op jit(solution)/shard_map/convert_element_type | solution.py:29
  53.9 1.4 %reshape.175 = f32[4,4,128,128]{3,2,1,0:T(8,128)S(1)} reshape(f32[1,4,8,1,8192]{4,2,1,3,0:T(8,128)} %copy.29) | data formatting | bytes 2097152 | tf_op jit(solution)/shard_map/convert_element_type | solution.py:29
  55.2 0.7 fusion.3
  56.0 1.5 %fusion = f32[4,4,1,128]{3,2,1,0:T(1,128)S(1)} fusion(f32[4,4,128,128]{3,2,1,0:T(8,128)S(1)} %reshape.175, f32[4,4,128]{2,1,0:T(4,128)S(1)} %get-tuple-element.15, f32[4,4,128]{2,1,0:T(4,128)S(1)} %get-tuple-element.11, f32[4,4,128]{2,1,0:T(4,128)S(1)} %get-tuple-element.7, f32[4,4,128]{2,1,0:T(4,128)S(1)} %get-tuple-element.12, ...), kind=kOutput, calls=%fused_computation.7 | convolution fusion | flops 2359296 | bytes 1110032 | tf_op jit(solution)/shard_map/rhk,rhkv->rhv/dot_general | solution.py:37
  57.4 2.4 %fusion.34 = f32[4,4,1,128]{3,2,1,0:T(1,128)S(1)} fusion(bf16[4,4,128,1]{2,1,0,3:T(4,128)(2,1)S(1)} %get-tuple-element.18, f32[4,4,128,128]{3,2,1,0:T(8,128)S(1)} %reshape.175, f32[4,4,128]{2,1,0:T(4,128)S(1)} %get-tuple-element.14, f32[4,4,128]{2,1,0:T(4,128)S(1)} %get-tuple-element.10, f32[4,4,128]{2,1,0:T(4,128)S(1)} %get-tuple-element.6, ...), kind=kOutput, calls=%fused_computation.67 | convolution fusion | flops 3145728 | bytes 1134608 | tf_op jit(solution)/shard_map/rhk,rhkv->rhv/dot_general | solution.py:37
  59.8 2.9 %fusion.2 = f32[4,4,1,128]{3,2,1,0:T(1,128)S(1)} fusion(f32[4,4,128]{2,1,0:T(4,128)S(1)} %get-tuple-element.13, f32[4,4,128]{2,1,0:T(4,128)S(1)} %get-tuple-element.9, f32[4,4,128]{2,1,0:T(4,128)S(1)} %get-tuple-element.5, bf16[4,4,128,1]{2,1,0,3:T(4,128)(2,1)S(1)} %get-tuple-element.17, f32[4,4,128,128]{3,2,1,0:T(8,128)S(1)} %reshape.175, ...), kind=kOutput, calls=%fused_computation.9 | convolution fusion | flops 3932160 | bytes 1159184 | tf_op jit(solution)/shard_map/rhk,rhkv->rhv/dot_general | solution.py:37
  62.7 0.1 fusion.29
  62.9 0.1 mul.212
  63.0 0.0 copy-done
  63.0 1.0 %fusion.30 = f32[16,2048]{1,0:T(8,128)} fusion(bf16[512,2048]{1,0:T(8,128)(2,1)S(1)} %copy-done, f32[16,512]{1,0:T(8,128)S(1)} %stack.32, f32[2,8,4,128]{3,2,1,0:T(4,128)S(1)} %bitcast.112, f32[512]{0:T(512)S(1)} %copy-done.6), kind=kOutput, calls=%fused_computation.51 | convolution fusion | flops 33579008 | bytes 2295808 | tf_op jit(solution)/shard_map/dot_general | solution.py:79
  64.0 0.0 all-reduce.2.cloned.1.call-update
  64.1 3.2 %fusion.1 = bf16[4,4,128,128]{3,2,1,0:T(8,128)(2,1)} fusion(f32[4,4,128]{2,1,0:T(4,128)S(1)} %get-tuple-element.13, f32[4,4,128]{2,1,0:T(4,128)S(1)} %get-tuple-element.9, f32[4,4,128]{2,1,0:T(4,128)S(1)} %get-tuple-element.5, f32[4,4,128]{2,1,0:T(4,128)S(1)} %get-tuple-element.14, f32[4,4,128]{2,1,0:T(4,128)S(1)} %get-tuple-element.10, ...), kind=kLoop, calls=%fused_computation.8 | loop fusion | flops 3670016 | bytes 1671184 | tf_op jit(solution)/shard_map/convert_element_type | solution.py:41
  67.3 27.5 %all-reduce.2.cloned.1.call-done = f32[16,2048]{1,0:T(8,128)} async-done(((f32[16,2048]{1,0:T(8,128)}), f32[16,2048]{1,0:T(8,128)}) %all-reduce.2.cloned.1.call-update) | async-done | bytes 131088 | tf_op jit(solution)/shard_map/psum | solution.py:80
  94.7 0.9 add_convert_fusion
  95.6 0.7 reshape.169
  (26 shorter events, 0.3 us)
Async XLA Ops:
  7.2 55.8 %copy-start = (bf16[512,2048]{1,0:T(8,128)(2,1)S(1)}, bf16[512,2048]{1,0:T(8,128)(2,1)}, u32[]{:S(2)}) copy-start(bf16[512,2048]{1,0:T(8,128)(2,1)} %param.19) | copy-start | bytes 6291460
  7.2 9.9 %copy-start.4 = (bf16[4,3,3,512]{3,0,2,1:T(4,128)(2,1)S(1)}, bf16[4,3,3,512]{3,0,2,1:T(4,128)(2,1)}, u32[]{:S(2)}) copy-start(bf16[4,3,3,512]{3,0,2,1:T(4,128)(2,1)} %param.12) | copy-start | bytes 110596
  7.2 10.0 %copy-start.3 = (bf16[4,3,512]{2,0,1:T(4,128)(2,1)S(1)}, bf16[4,3,512]{2,0,1:T(4,128)(2,1)}, u32[]{:S(2)}) copy-start(bf16[4,3,512]{2,0,1:T(4,128)(2,1)} %param.13) | copy-start | bytes 36868
  7.2 10.0 %copy-start.7 = (s32[32]{0:T(128)S(1)}, s32[32]{0:T(128)}, u32[]{:S(2)}) copy-start(s32[32]{0:T(128)} %param.16) | copy-start | bytes 388
  7.2 10.2 %copy-start.2 = (bf16[4,4,3,512]{3,1,2,0:T(4,128)(2,1)S(1)}, bf16[4,4,3,512]{3,1,2,0:T(4,128)(2,1)}, u32[]{:S(2)}) copy-start(bf16[4,4,3,512]{3,1,2,0:T(4,128)(2,1)} %param.11) | copy-start | bytes 147460
  7.2 10.4 %copy-start.8 = (s32[32]{0:T(128)S(1)}, s32[32]{0:T(128)}, u32[]{:S(2)}) copy-start(s32[32]{0:T(128)} %param.15) | copy-start | bytes 388
  7.2 11.3 %copy-start.5 = (f32[512]{0:T(512)S(1)}, f32[512]{0:T(512)}, u32[]{:S(2)}) copy-start(f32[512]{0:T(512)} %param.14) | copy-start | bytes 6148
  9.8 21.7 %all-to-all-start = ((bf16[4,8,8192]{2,0,1:T(4,128)(2,1)}), bf16[4,8,8192]{2,0,1:T(4,128)(2,1)S(1)}, u32[]{:S(2)}, u32[]{:S(2)}) async-start(bf16[4,8,8192]{2,0,1:T(4,128)(2,1)} %copy.27), calls=%async_computation | async-start | bytes 1048576 | tf_op jit(solution)/shard_map/all_to_all | solution.py:68
  32.6 5.0 %copy-start.1 = (bf16[4,4,2048]{2,1,0:T(4,128)(2,1)S(1)}, bf16[4,4,2048]{2,1,0:T(4,128)(2,1)}, u32[]{:S(2)}) copy-start(bf16[4,4,2048]{2,1,0:T(4,128)(2,1)} %param.10) | copy-start | bytes 196612
  33.9 18.3 %all-to-all-start.1 = ((bf16[8,4,1,8192]{3,1,2,0:T(4,128)(2,1)}), bf16[8,4,1,8192]{3,1,2,0:T(4,128)(2,1)S(1)}, u32[]{:S(2)}, u32[]{:S(2)}) async-start(bf16[8,4,1,8192]{3,1,2,0:T(4,128)(2,1)} %bitcast_select_fusion), calls=%async_computation.1 | async-start | bytes 1048576 | tf_op jit(solution)/shard_map/all_to_all | solution.py:72
  37.5 57.2 %all-reduce.2.cloned.1.call-start = ((), (), s32[]{:S(2)}) async-start(), calls=%async_computation.2 | async-start | bytes 262144 | tf_op jit(solution)/shard_map/psum | solution.py:80
  59.8 3.2 %copy-start.6 = (f32[512]{0:T(512)S(1)}, f32[512]{0:T(512)}, u32[]{:S(2)}) copy-start(f32[512]{0:T(512)} %param.18) | copy-start | bytes 6148
Sparse Core Ops, SparseCore 0:
  64.2 30.4 all-reduce.1
where the time goes:
time: 103 us
  waiting for transfers between devices  55 us (53%)
  between operations  14.4 us (14%)
  starting transfers between devices  10.9 us (11%)
  matrix products  8.49 us (8%)
  local copies, waits for them, and re-layouts  8.43 us (8%)
  other arithmetic  5.91 us (6%)
    psum x1, waiting for transfers between devices, body(): summed = lax.psum(partial_value, 'head')  27.5 us
    all_to_all x1, waiting for transfers between devices, body(): lax.all_to_all(picked, 'req', split_axis=0, concat_axis=2, tiled=True)  14.5 us
    all_to_all x1, waiting for transfers between devices, body(): lax.all_to_all(pieces, 'req', split_axis=1, concat_axis=0, tiled=True)  13 us
    dot_general x4, matrix products, recurrence(): outputs.append(jnp.einsum('rhk,rhkv->rhv', queries[:, position], current))  7.46 us
    all_to_all x1, starting transfers between devices, body(): lax.all_to_all(pieces, 'req', split_axis=1, concat_axis=0, tiled=True)  7.25 us
    all_to_all x1, starting transfers between devices, body(): lax.all_to_all(picked, 'req', split_axis=0, concat_axis=2, tiled=True)  3.64 us
    convert_element_type x1, other arithmetic, recurrence(): return (normed.astype(jnp.bfloat16), current.astype(jnp.bfloat16))  3.19 us
    convert_element_type x2, local copies, waits for them, and re-layouts, recurrence(): relocated.astype(jnp.float32)  2.97 us
  transfers between devices with their start and end apart: 3, of which 3 were waited for; matrix products, arithmetic and copies ran while one was open for 4% of the time, Pallas kernels for 0%

commit v1 on v0

--- a/solution.py
+++ b/solution.py
@@ -69,7 +69,10 @@
         total_reqs, -1
     )
     picked = jnp.take(spread, inverse, axis=0).reshape(devices, local_reqs, 1, -1)
-    routed = lax.all_to_all(picked, "req", split_axis=0, concat_axis=2, tiled=True)
+    routed = jnp.concatenate(
+        lax.all_to_all(jnp.stack(jnp.split(picked, lax.axis_size("req"), axis=0)), "req", 0, 0),
+        axis=2,
+    )
     relocated = routed.reshape(old_state.shape)
     normed, new_state = recurrence(
         convolved, relocated, local_lens, forget_bias, norm_gain, head_size

time: 103 us -> 108 us (1.049)
  local copies, waits for them, and re-layouts: 8.43 us -> 13.4 us
    unnamed x21 -> x28, local copies, waits for them, and re-layouts: 0.07 us -> 4.67 us
where the time goes in v1:
time: 108 us; the launch traced here: 107 us
  waiting for transfers between devices  55.1 us (51%)
  between operations  14.4 us (13%)
  local copies, waits for them, and re-layouts  13.4 us (12%)
  starting transfers between devices  10.9 us (10%)
  matrix products  8.49 us (8%)
  other arithmetic  4.93 us (5%)
    psum x1, waiting for transfers between devices, body(): summed = lax.psum(partial_value, 'head')  27.5 us
    all_to_all x1, waiting for transfers between devices, body(): lax.all_to_all(jnp.stack(jnp.split(picked, lax.axis_size('req'), axis=0))...  14.5 us
    all_to_all x1, waiting for transfers between devices, body(): lax.all_to_all(pieces, 'req', split_axis=1, concat_axis=0, tiled=True)  13.1 us
    dot_general x4, matrix products, recurrence(): outputs.append(jnp.einsum('rhk,rhkv->rhv', queries[:, position], current))  7.46 us
    all_to_all x1, starting transfers between devices, body(): lax.all_to_all(pieces, 'req', split_axis=1, concat_axis=0, tiled=True)  7.25 us
    unnamed x28, local copies, waits for them, and re-layouts  4.67 us
    all_to_all x1, starting transfers between devices, body(): lax.all_to_all(jnp.stack(jnp.split(picked, lax.axis_size('req'), axis=0))...  3.64 us
    convert_element_type x1, other arithmetic, recurrence(): return (normed.astype(jnp.bfloat16), current.astype(jnp.bfloat16))  3.19 us
  transfers between devices with their start and end apart: 3, of which 3 were waited for; matrix products, arithmetic and copies ran while one was open for 4% of the time, Pallas kernels for 0%

profile of v1, /device:TPU:0, one launch (start us, length us, event | category | flops | bytes accessed | tf_op | source)
XLA Modules:
  0.0 107.2 jit_solution(11914338614993647465)
XLA Ops:
  7.2 0.0 copy-start
  7.2 0.0 copy-start.8
  7.2 0.0 copy-start.4
  7.2 0.0 copy-start.3
  7.2 0.0 copy-start.7
  7.2 0.0 copy-start.2
  7.2 0.0 copy-start.5
  7.2 1.4 %reshape.163 = bf16[4,8,8192]{2,1,0:T(8,128)(2,1)S(1)} reshape(bf16[4,4,128,128]{3,2,1,0:T(8,128)(2,1)} %param.17) | data formatting | bytes 1048576 | tf_op jit(solution)/shard_map/reshape | solution.py:67
  8.6 1.2 %copy.21 = bf16[4,8,8192]{2,0,1:T(4,128)(2,1)} copy(bf16[4,8,8192]{2,1,0:T(8,128)(2,1)S(1)} %reshape.163) | data formatting | bytes 1048576 | tf_op jit(solution)/shard_map/reshape | solution.py:67
  9.8 7.3 %all-to-all-start = ((bf16[4,8,8192]{2,0,1:T(4,128)(2,1)}), bf16[4,8,8192]{2,0,1:T(4,128)(2,1)S(1)}, u32[]{:S(2)}, u32[]{:S(2)}) async-start(bf16[4,8,8192]{2,0,1:T(4,128)(2,1)} %copy.21), calls=%async_computation | async-start | bytes 1048576 | tf_op jit(solution)/shard_map/all_to_all | solution.py:68
  17.1 0.0 copy-done.8
  17.1 0.7 scatter_custom_fusion
  17.9 0.1 compare_convert_fusion
  18.0 0.1 add_compare_fusion
  18.1 0.1 convert_select_fusion
  18.2 0.1 fusion.21
  18.5 13.1 %all-to-all-done = bf16[4,8,8192]{2,0,1:T(4,128)(2,1)S(1)} async-done(((bf16[4,8,8192]{2,0,1:T(4,128)(2,1)}), bf16[4,8,8192]{2,0,1:T(4,128)(2,1)S(1)}, u32[]{:S(2)}, u32[]{:S(2)}) %all-to-all-start) | async-done | bytes 524320 | tf_op jit(solution)/shard_map/all_to_all | solution.py:68
  31.6 0.1 reshape.164
  31.7 0.9 gather_fusion
  32.6 0.0 copy-start.1
  32.6 0.1 broadcast_select_fusion
  32.7 0.6 fusion.29
  33.4 0.7 fusion.28
  34.0 0.6 fusion.27
  34.7 0.7 fusion.26
  35.4 0.6 fusion.25
  36.0 0.7 fusion.24
  36.7 0.6 fusion.23
  37.3 0.7 fusion.22
  38.0 3.6 %all-to-all-start.1 = ((bf16[8,1,4,1,8192]{4,2,3,1,0:T(4,128)(2,1)}), bf16[8,1,4,1,8192]{4,2,3,1,0:T(4,128)(2,1)S(1)}, u32[]{:S(2)}, u32[]{:S(2)}) async-start(bf16[8,1,4,1,8192]{4,2,3,1,0:T(4,128)(2,1)} %fusion.22), calls=%async_computation.1 | async-start | bytes 1048576 | tf_op jit(solution)/shard_map/all_to_all | solution.py:73
  41.6 0.0 all-reduce.2.cloned.1.call-start
  41.8 14.5 %all-to-all-done.1 = bf16[8,1,4,1,8192]{4,2,3,1,0:T(4,128)(2,1)S(1)} async-done(((bf16[8,1,4,1,8192]{4,2,3,1,0:T(4,128)(2,1)}), bf16[8,1,4,1,8192]{4,2,3,1,0:T(4,128)(2,1)S(1)}, u32[]{:S(2)}, u32[]{:S(2)}) %all-to-all-start.1) | async-done | bytes 524320 | tf_op jit(solution)/shard_map/all_to_all | solution.py:73
  56.3 0.1 convert_bitcast_fusion
  56.4 1.6 %copy.22 = f32[1,4,8,1,8192]{4,2,1,3,0:T(8,128)} copy(f32[1,4,8,1,8192]{4,1,3,0,2:T(4,128)S(1)} %convert_bitcast_fusion) | data formatting | bytes 2097152 | tf_op jit(solution)/shard_map/convert_element_type | solution.py:29
  58.0 1.4 %reshape.171 = f32[4,4,128,128]{3,2,1,0:T(8,128)S(1)} reshape(f32[1,4,8,1,8192]{4,2,1,3,0:T(8,128)} %copy.22) | data formatting | bytes 2097152 | tf_op jit(solution)/shard_map/convert_element_type | solution.py:29
  59.3 0.7 fusion.3
  60.1 1.5 %fusion = f32[4,4,1,128]{3,2,1,0:T(1,128)S(1)} fusion(f32[4,4,128,128]{3,2,1,0:T(8,128)S(1)} %reshape.171, f32[4,4,128]{2,1,0:T(4,128)S(1)} %get-tuple-element.15, f32[4,4,128]{2,1,0:T(4,128)S(1)} %get-tuple-element.11, f32[4,4,128]{2,1,0:T(4,128)S(1)} %get-tuple-element.7, f32[4,4,128]{2,1,0:T(4,128)S(1)} %get-tuple-element.12, ...), kind=kOutput, calls=%fused_computation.7 | convolution fusion | flops 2359296 | bytes 1110032 | tf_op jit(solution)/shard_map/rhk,rhkv->rhv/dot_general | solution.py:37
  61.5 2.4 %fusion.42 = f32[4,4,1,128]{3,2,1,0:T(1,128)S(1)} fusion(bf16[4,4,128,1]{2,1,0,3:T(4,128)(2,1)S(1)} %get-tuple-element.18, f32[4,4,128,128]{3,2,1,0:T(8,128)S(1)} %reshape.171, f32[4,4,128]{2,1,0:T(4,128)S(1)} %get-tuple-element.14, f32[4,4,128]{2,1,0:T(4,128)S(1)} %get-tuple-element.10, f32[4,4,128]{2,1,0:T(4,128)S(1)} %get-tuple-element.6, ...), kind=kOutput, calls=%fused_computation.83 | convolution fusion | flops 3145728 | bytes 1134608 | tf_op jit(solution)/shard_map/rhk,rhkv->rhv/dot_general | solution.py:37
  63.9 2.9 %fusion.2 = f32[4,4,1,128]{3,2,1,0:T(1,128)S(1)} fusion(f32[4,4,128]{2,1,0:T(4,128)S(1)} %get-tuple-element.13, f32[4,4,128]{2,1,0:T(4,128)S(1)} %get-tuple-element.9, f32[4,4,128]{2,1,0:T(4,128)S(1)} %get-tuple-element.5, bf16[4,4,128,1]{2,1,0,3:T(4,128)(2,1)S(1)} %get-tuple-element.17, f32[4,4,128,128]{3,2,1,0:T(8,128)S(1)} %reshape.171, ...), kind=kOutput, calls=%fused_computation.9 | convolution fusion | flops 3932160 | bytes 1159184 | tf_op jit(solution)/shard_map/rhk,rhkv->rhv/dot_general | solution.py:37
  66.8 0.1 fusion.37
  67.0 0.1 mul.212
  67.1 0.0 copy-done
  67.1 1.0 fusion.38
  68.1 0.0 all-reduce.2.cloned.1.call-update
  68.2 3.2 %fusion.1 = bf16[4,4,128,128]{3,2,1,0:T(8,128)(2,1)} fusion(f32[4,4,128]{2,1,0:T(4,128)S(1)} %get-tuple-element.13, f32[4,4,128]{2,1,0:T(4,128)S(1)} %get-tuple-element.9, f32[4,4,128]{2,1,0:T(4,128)S(1)} %get-tuple-element.5, f32[4,4,128]{2,1,0:T(4,128)S(1)} %get-tuple-element.14, f32[4,4,128]{2,1,0:T(4,128)S(1)} %get-tuple-element.10, ...), kind=kLoop, calls=%fused_computation.8 | loop fusion | flops 3670016 | bytes 1671184 | tf_op jit(solution)/shard_map/convert_element_type | solution.py:41
  71.3 27.5 %all-reduce.2.cloned.1.call-done = f32[16,2048]{1,0:T(8,128)} async-done(((f32[16,2048]{1,0:T(8,128)}), f32[16,2048]{1,0:T(8,128)}) %all-reduce.2.cloned.1.call-update) | async-done | bytes 131088 | tf_op jit(solution)/shard_map/psum | solution.py:83
  98.8 0.9 add_convert_fusion
  99.7 0.7 reshape.165
  (32 shorter events, 0.3 us)
Async XLA Ops:
  7.2 59.9 %copy-start = (bf16[512,2048]{1,0:T(8,128)(2,1)S(1)}, bf16[512,2048]{1,0:T(8,128)(2,1)}, u32[]{:S(2)}) copy-start(bf16[512,2048]{1,0:T(8,128)(2,1)} %param.19) | copy-start | bytes 6291460
  7.2 9.9 %copy-start.8 = (s32[32]{0:T(128)S(1)}, s32[32]{0:T(128)}, u32[]{:S(2)}) copy-start(s32[32]{0:T(128)} %param.15) | copy-start | bytes 388
  7.2 10.6 %copy-start.4 = (bf16[4,3,3,512]{3,0,2,1:T(4,128)(2,1)S(1)}, bf16[4,3,3,512]{3,0,2,1:T(4,128)(2,1)}, u32[]{:S(2)}) copy-start(bf16[4,3,3,512]{3,0,2,1:T(4,128)(2,1)} %param.12) | copy-start | bytes 110596
  7.2 10.7 %copy-start.3 = (bf16[4,3,512]{2,0,1:T(4,128)(2,1)S(1)}, bf16[4,3,512]{2,0,1:T(4,128)(2,1)}, u32[]{:S(2)}) copy-start(bf16[4,3,512]{2,0,1:T(4,128)(2,1)} %param.13) | copy-start | bytes 36868
  7.2 10.7 %copy-start.7 = (s32[32]{0:T(128)S(1)}, s32[32]{0:T(128)}, u32[]{:S(2)}) copy-start(s32[32]{0:T(128)} %param.16) | copy-start | bytes 388
  7.2 10.9 %copy-start.2 = (bf16[4,4,3,512]{3,1,2,0:T(4,128)(2,1)S(1)}, bf16[4,4,3,512]{3,1,2,0:T(4,128)(2,1)}, u32[]{:S(2)}) copy-start(bf16[4,4,3,512]{3,1,2,0:T(4,128)(2,1)} %param.11) | copy-start | bytes 147460
  7.2 11.2 %copy-start.5 = (f32[512]{0:T(512)S(1)}, f32[512]{0:T(512)}, u32[]{:S(2)}) copy-start(f32[512]{0:T(512)} %param.14) | copy-start | bytes 6148
  9.8 21.7 %all-to-all-start = ((bf16[4,8,8192]{2,0,1:T(4,128)(2,1)}), bf16[4,8,8192]{2,0,1:T(4,128)(2,1)S(1)}, u32[]{:S(2)}, u32[]{:S(2)}) async-start(bf16[4,8,8192]{2,0,1:T(4,128)(2,1)} %copy.21), calls=%async_computation | async-start | bytes 1048576 | tf_op jit(solution)/shard_map/all_to_all | solution.py:68
  32.6 9.1 %copy-start.1 = (bf16[4,4,2048]{2,1,0:T(4,128)(2,1)S(1)}, bf16[4,4,2048]{2,1,0:T(4,128)(2,1)}, u32[]{:S(2)}) copy-start(bf16[4,4,2048]{2,1,0:T(4,128)(2,1)} %param.10) | copy-start | bytes 196612
  38.0 18.3 %all-to-all-start.1 = ((bf16[8,1,4,1,8192]{4,2,3,1,0:T(4,128)(2,1)}), bf16[8,1,4,1,8192]{4,2,3,1,0:T(4,128)(2,1)S(1)}, u32[]{:S(2)}, u32[]{:S(2)}) async-start(bf16[8,1,4,1,8192]{4,2,3,1,0:T(4,128)(2,1)} %fusion.22), calls=%async_computation.1 | async-start | bytes 1048576 | tf_op jit(solution)/shard_map/all_to_all | solution.py:73
  41.6 57.2 %all-reduce.2.cloned.1.call-start = ((), (), s32[]{:S(2)}) async-start(), calls=%async_computation.2 | async-start | bytes 262144 | tf_op jit(solution)/shard_map/psum | solution.py:83
  63.9 3.2 %copy-start.6 = (f32[512]{0:T(512)S(1)}, f32[512]{0:T(512)}, u32[]{:S(2)}) copy-start(f32[512]{0:T(512)} %param.18) | copy-start | bytes 6148
Sparse Core Ops, SparseCore 0:
  68.3 30.4 all-reduce.1
